TPU v7x, 32 devices: a whole 2x2x4 slice. The times are simulated.
32 devices in a mesh: dp: 8 (over z, y), tensor: 4 (over x, core).
Axes of the slice: x: 2, y: 2, z: 4, core: 2. Of those that a mesh axis runs over, the one named last changes fastest.
Arguments:
- tokens: bfloat16 [2048, 1024], P('dp'), may hold values from -6 to 6
- norm_gain: float32 [1024], replicated, may hold values from 0.25 to 1.75
- w_query: bfloat16 [1024, 1024], P(None, 'tensor'), may hold values from -0.1875 to 0.1875
- w_key: bfloat16 [1024, 1024], P(None, 'tensor'), may hold values from -0.1875 to 0.1875
- w_value: bfloat16 [1024, 2048], P(None, 'tensor'), may hold values from -0.1875 to 0.1875
- w_outgate: bfloat16 [1024, 2048], P(None, 'tensor'), may hold values from -0.1875 to 0.1875
- w_decay: bfloat16 [1024, 8], P(None, 'tensor'), may hold values from -0.1875 to 0.1875
- w_beta: bfloat16 [1024, 8], P(None, 'tensor'), may hold values from -0.1875 to 0.1875
- conv_query: float32 [4, 1024], P(None, 'tensor'), may hold values from -3 to 3
- conv_key: float32 [4, 1024], P(None, 'tensor'), may hold values from -3 to 3
- conv_value: float32 [4, 2048], P(None, 'tensor'), may hold values from -3 to 3
- decay_log: float32 [8], P('tensor'), may hold values from -6 to 0.5
- decay_bias: float32 [8], P('tensor'), may hold values from -1 to 1
- out_norm_gain: float32 [256], replicated, may hold values from 0.25 to 1.75
- w_out: bfloat16 [1024, 2048], P(None, 'tensor'), may hold values from -0.125 to 0.125
- ffn_gain: float32 [1024], replicated, may hold values from 0.25 to 1.75
- w_gate: bfloat16 [1024, 2816], P(None, 'tensor'), may hold values from -0.1875 to 0.1875
- w_up: bfloat16 [1024, 2816], P(None, 'tensor'), may hold values from -0.1875 to 0.1875
- w_down: bfloat16 [1024, 2816], P(None, 'tensor'), may hold values from -0.109375 to 0.109375
- cotangent: bfloat16 [2048, 1024], P('dp'), may hold values from -6 to 6
Outputs:
- layer_out: float32 [2048, 1024], P('dp', 'tensor')
- grad_input: float32 [2048, 1024], P('dp', 'tensor')
- grad_norm_gain: float32 [1024], replicated
- grad_query: float32 [1024, 1024], P('dp', 'tensor')
- grad_key: float32 [1024, 1024], P('dp', 'tensor')
- grad_value: float32 [1024, 2048], P('dp', 'tensor')
- grad_outgate: float32 [1024, 2048], P('dp', 'tensor')
- grad_decay: float32 [1024, 8], P('dp', 'tensor')
- grad_beta: float32 [1024, 8], P('dp', 'tensor')
- grad_conv_query: float32 [4, 1024], P(None, 'tensor')
- grad_conv_key: float32 [4, 1024], P(None, 'tensor')
- grad_conv_value: float32 [4, 2048], P(None, 'tensor')
- grad_decay_log: float32 [8], P('tensor')
- grad_decay_bias: float32 [8], P('tensor')
- grad_out_norm_gain: float32 [256], replicated
- grad_out: float32 [1024, 2048], P('dp', 'tensor')
- grad_ffn_gain: float32 [1024], replicated
- grad_gate: float32 [1024, 2816], P('dp', 'tensor')
- grad_up: float32 [1024, 2816], P('dp', 'tensor')
- grad_down: float32 [1024, 2816], P('dp', 'tensor')
All inputs are finite; a program needn't handle non-finite values.
Results may differ from a plain program's by a relative error of at most 0.012.
Values sent between devices are 32-bit elements; how exact they have to be, the bound alone decides.
No kernel may reach another device: no remote copies, remote signals or barrier semaphores. Data moves between devices by JAX's collectives and lax.ppermute only.
A program may use at most 128 MiB of HBM per device.

v0:
```python
import jax
import jax.numpy as jnp
from jax import lax
from jax.sharding import PartitionSpec as P

GROUP = 64
EPSILON = 1e-06
HIGH = lax.Precision.HIGHEST


def causal_conv(signal, taps):
    length = signal.shape[0]
    count = taps.shape[0]
    padded = jnp.concatenate([jnp.zeros((count - 1, signal.shape[1]), jnp.float32), signal], axis=0)
    total = taps[0] * padded[0:length]
    for index in range(1, count):
        total = total + taps[index] * padded[index : index + length]
    return total


def head_norm(signal, heads):
    shaped = signal.reshape(signal.shape[0], heads, -1)
    return shaped * lax.rsqrt(jnp.sum(shaped * shaped, axis=2, keepdims=True) + EPSILON)


def delta_rule(query, keys, values, beta, logdecay, block):
    length, heads, kdim = keys.shape
    vdim = values.shape[2]
    blocks = length // block
    position = jnp.arange(block)
    lower = (position[:, None] >= position[None, :])[:, :, None]
    strict = (position[:, None] > position[None, :])[:, :, None]
    identity = jnp.eye(block, dtype=jnp.float32)[None]
    squares = block.bit_length() - 2

    def step(state, inputs):
        qblk, kblk, vblk, bblk, gblk = inputs
        cumul = jnp.cumsum(gblk, axis=0)
        ratio = jnp.exp(jnp.where(lower, cumul[:, None, :] - cumul[None, :, :], -1e30))
        growth = jnp.exp(cumul)
        tail = jnp.exp(cumul[-1][None, :] - cumul)
        keykey = jnp.einsum("thd,shd->tsh", kblk, kblk, precision=HIGH)
        strong = jnp.where(strict, keykey * ratio * bblk[:, None, :], 0.0)
        known = jnp.einsum("thd,hed->the", kblk, state, precision=HIGH)
        target = bblk[:, :, None] * (vblk - growth[:, :, None] * known)
        matrix = jnp.transpose(strong, (2, 0, 1))
        inverse = identity - matrix
        power = matrix
        for count in range(squares):
            power = jnp.einsum("hij,hjk->hik", power, power, precision=HIGH)
            inverse = jnp.einsum("hij,hjk->hik", inverse, identity + power, precision=HIGH)
        fresh = jnp.einsum("hts,she->hte", inverse, target, precision=HIGH)
        scores = jnp.where(
            lower, jnp.einsum("thd,shd->tsh", qblk, kblk, precision=HIGH) * ratio, 0.0
        )
        result = growth[:, :, None] * jnp.einsum("thd,hed->the", qblk, state, precision=HIGH)
        result = result + jnp.einsum("tsh,hse->the", scores, fresh, precision=HIGH)
        weighted = tail[:, :, None] * kblk
        new_state = growth[-1][:, None, None] * state + jnp.einsum(
            "hse,shd->hed", fresh, weighted, precision=HIGH
        )
        return (new_state, result)

    start = jnp.zeros((heads, vdim, kdim), jnp.float32)
    inputs = (
        query.reshape(blocks, block, heads, kdim),
        keys.reshape(blocks, block, heads, kdim),
        values.reshape(blocks, block, heads, vdim),
        beta.reshape(blocks, block, heads),
        logdecay.reshape(blocks, block, heads),
    )
    final, results = lax.scan(step, start, inputs)
    return results.reshape(length, heads * vdim)


def mixer(qlin, klin, vlin, alin, blin, conv_q, conv_k, conv_v, rate_log, rate_bias):
    heads = rate_log.shape[0]
    length = qlin.shape[0]
    kdim = qlin.shape[1] // heads
    query = head_norm(jax.nn.silu(causal_conv(qlin, conv_q)), heads) * kdim ** (-0.5)
    keys = head_norm(jax.nn.silu(causal_conv(klin, conv_k)), heads)
    values = jax.nn.silu(causal_conv(vlin, conv_v)).reshape(length, heads, -1)
    beta = jax.nn.sigmoid(blin)
    logdecay = -jnp.exp(rate_log) * jax.nn.softplus(alin + rate_bias)
    return delta_rule(query, keys, values, beta, logdecay, GROUP)


def gated_norm(mixed, zlin, gain):
    length = mixed.shape[0]
    vdim = gain.shape[0]
    shaped = mixed.reshape(length, -1, vdim)
    scale = lax.rsqrt(jnp.mean(shaped * shaped, axis=2, keepdims=True) + EPSILON)
    gates = jax.nn.silu(zlin).reshape(length, -1, vdim)
    return (shaped * scale * gain * gates).reshape(length, -1)


def rms_back(grad_normed, unit, inverse_rms, gain):
    scaled = grad_normed * gain
    return inverse_rms * (scaled - unit * jnp.mean(scaled * unit, axis=1, keepdims=True))


def project(operand, weights):
    return jnp.dot(operand, weights, preferred_element_type=jnp.float32)


def back_dot(operand, weights):
    return jnp.einsum("tc,dc->td", operand, weights, preferred_element_type=jnp.float32)


def outer_sum(operand, other):
    return jnp.einsum("td,tc->dc", operand, other, preferred_element_type=jnp.float32)


def local(
    tokens,
    norm_gain,
    w_query,
    w_key,
    w_value,
    w_outgate,
    w_decay,
    w_beta,
    conv_query,
    conv_key,
    conv_value,
    decay_log,
    decay_bias,
    out_norm_gain,
    w_out,
    ffn_gain,
    w_gate,
    w_up,
    w_down,
    cotangent,
):
    inputs = tokens.astype(jnp.float32)
    inv_first = lax.rsqrt(jnp.mean(inputs * inputs, axis=1, keepdims=True) + EPSILON)
    unit_first = inputs * inv_first
    normed_first = (unit_first * norm_gain).astype(jnp.bfloat16)
    qlin = project(normed_first, w_query)
    klin = project(normed_first, w_key)
    vlin = project(normed_first, w_value)
    zlin = project(normed_first, w_outgate)
    alin = project(normed_first, w_decay)
    blin = project(normed_first, w_beta)
    mixed, mixer_grads_fn = jax.vjp(
        mixer, qlin, klin, vlin, alin, blin, conv_query, conv_key, conv_value, decay_log, decay_bias
    )
    gated, gated_back = jax.vjp(gated_norm, mixed, zlin, out_norm_gain)
    gated_bf = gated.astype(jnp.bfloat16)
    mixer_part = back_dot(gated_bf, w_out)
    resid = inputs + lax.psum(mixer_part, "tensor")
    inv_second = lax.rsqrt(jnp.mean(resid * resid, axis=1, keepdims=True) + EPSILON)
    unit_second = resid * inv_second
    normed_second = (unit_second * ffn_gain).astype(jnp.bfloat16)
    glin = project(normed_second, w_gate)
    ulin = project(normed_second, w_up)
    sigm = jax.nn.sigmoid(glin)
    silu_gate = glin * sigm
    hidden = (silu_gate * ulin).astype(jnp.bfloat16)
    ffn_part = back_dot(hidden, w_down)
    width = resid.shape[1] // lax.axis_size("tensor")
    offset = lax.axis_index("tensor") * width
    ffn_share = lax.psum_scatter(ffn_part, "tensor", scatter_dimension=1, tiled=True)
    layer_out = lax.dynamic_slice_in_dim(resid, offset, width, 1) + ffn_share
    dhidden = project(cotangent, w_down)
    grad_down = outer_sum(cotangent, hidden)
    dglin = (dhidden * ulin * sigm * (1.0 + glin * (1.0 - sigm))).astype(jnp.bfloat16)
    dulin = (dhidden * silu_gate).astype(jnp.bfloat16)
    grad_gate = outer_sum(normed_second, dglin)
    grad_up = outer_sum(normed_second, dulin)
    second_part = back_dot(dglin, w_gate) + back_dot(dulin, w_up)
    dnormed2 = lax.psum(second_part, "tensor")
    grad_ffn_gain = jnp.sum(dnormed2 * unit_second, axis=0)
    dresid = cotangent.astype(jnp.float32) + rms_back(dnormed2, unit_second, inv_second, ffn_gain)
    dresid_bf = dresid.astype(jnp.bfloat16)
    grad_out = outer_sum(dresid_bf, gated_bf)
    dgated = project(dresid_bf, w_out)
    dmixed, dzlin, grad_out_norm = gated_back(dgated)
    dqlin, dklin, dvlin, dalin, dblin, grad_cq, grad_ck, grad_cv, grad_dlog, grad_dbias = (
        mixer_grads_fn(dmixed)
    )
    dq_bf = dqlin.astype(jnp.bfloat16)
    dk_bf = dklin.astype(jnp.bfloat16)
    dv_bf = dvlin.astype(jnp.bfloat16)
    dz_bf = dzlin.astype(jnp.bfloat16)
    da_bf = dalin.astype(jnp.bfloat16)
    db_bf = dblin.astype(jnp.bfloat16)
    grad_query = outer_sum(normed_first, dq_bf)
    grad_key = outer_sum(normed_first, dk_bf)
    grad_value = outer_sum(normed_first, dv_bf)
    grad_outgate = outer_sum(normed_first, dz_bf)
    grad_decay = outer_sum(normed_first, da_bf)
    grad_beta = outer_sum(normed_first, db_bf)
    first_part = (
        back_dot(dq_bf, w_query)
        + back_dot(dk_bf, w_key)
        + back_dot(dv_bf, w_value)
        + back_dot(dz_bf, w_outgate)
        + back_dot(da_bf, w_decay)
        + back_dot(db_bf, w_beta)
    )
    dnormed1, out_norm_total = lax.psum((first_part, grad_out_norm), "tensor")
    grad_norm_gain = jnp.sum(dnormed1 * unit_first, axis=0)
    grad_rows = dresid + rms_back(dnormed1, unit_first, inv_first, norm_gain)
    grad_input = lax.dynamic_slice_in_dim(grad_rows, offset, width, 1)
    sum_norm_gain, sum_ffn_gain, sum_out_norm, sum_dlog, sum_dbias, sum_cq, sum_ck, sum_cv = (
        lax.psum(
            (
                grad_norm_gain,
                grad_ffn_gain,
                out_norm_total,
                grad_dlog,
                grad_dbias,
                grad_cq,
                grad_ck,
                grad_cv,
            ),
            "dp",
        )
    )
    (
        sum_query,
        sum_key,
        sum_value,
        sum_outgate,
        sum_decay,
        sum_beta,
        sum_out,
        sum_gate,
        sum_up,
        sum_down,
    ) = (
        lax.psum_scatter(grad_query, "dp", scatter_dimension=0, tiled=True),
        lax.psum_scatter(grad_key, "dp", scatter_dimension=0, tiled=True),
        lax.psum_scatter(grad_value, "dp", scatter_dimension=0, tiled=True),
        lax.psum_scatter(grad_outgate, "dp", scatter_dimension=0, tiled=True),
        lax.psum_scatter(grad_decay, "dp", scatter_dimension=0, tiled=True),
        lax.psum_scatter(grad_beta, "dp", scatter_dimension=0, tiled=True),
        lax.psum_scatter(grad_out, "dp", scatter_dimension=0, tiled=True),
        lax.psum_scatter(grad_gate, "dp", scatter_dimension=0, tiled=True),
        lax.psum_scatter(grad_up, "dp", scatter_dimension=0, tiled=True),
        lax.psum_scatter(grad_down, "dp", scatter_dimension=0, tiled=True),
    )
    return (
        layer_out,
        grad_input,
        sum_norm_gain,
        sum_query,
        sum_key,
        sum_value,
        sum_outgate,
        sum_decay,
        sum_beta,
        sum_cq,
        sum_ck,
        sum_cv,
        sum_dlog,
        sum_dbias,
        sum_out_norm,
        sum_out,
        sum_ffn_gain,
        sum_gate,
        sum_up,
        sum_down,
    )


def solution(mesh):
    return jax.shard_map(
        local,
        mesh=mesh,
        in_specs=(
            P("dp", None),
            P(),
            P(None, "tensor"),
            P(None, "tensor"),
            P(None, "tensor"),
            P(None, "tensor"),
            P(None, "tensor"),
            P(None, "tensor"),
            P(None, "tensor"),
            P(None, "tensor"),
            P(None, "tensor"),
            P("tensor"),
            P("tensor"),
            P(),
            P(None, "tensor"),
            P(),
            P(None, "tensor"),
            P(None, "tensor"),
            P(None, "tensor"),
            P("dp", None),
        ),
        out_specs=(
            P("dp", "tensor"),
            P("dp", "tensor"),
            P(),
            P("dp", "tensor"),
            P("dp", "tensor"),
            P("dp", "tensor"),
            P("dp", "tensor"),
            P("dp", "tensor"),
            P("dp", "tensor"),
            P(None, "tensor"),
            P(None, "tensor"),
            P(None, "tensor"),
            P("tensor"),
            P("tensor"),
            P(),
            P("dp", "tensor"),
            P(),
            P("dp", "tensor"),
            P("dp", "tensor"),
            P("dp", "tensor"),
        ),
        check_vma=False,
    )
```

profile of v0, /device:TPU:0, one launch (start us, length us, event | category | flops | bytes accessed | tf_op | source)
XLA Modules:
  0.0 1246.9 jit_solution(6733757201012686613)
XLA Ops:
  17.2 1.7 fusion.305
  24.9 95.7 %while.116 = (s32[]{:T(128)}, f32[2,256,128]{2,1,0:T(8,128)S(1)}, f32[4,64,2,256]{3,1,2,0:T(8,128)}, f32[4,64,64,2]{1,2,3,0:T(8,128)}, f32[4,64,2]{1,2,0:T(2,128...) while((s32[]{:T(128)}, f32[2,256,128]{2,1,0:T(8,128)S(1)}, ...), condition=%wide.region_5.6_spmd.clone.clone, body=%wide.region_3.5_spmd.clone.clone.sunk | while | flops 290349312 | bytes 8199534 | solution.py:72
  41.0 1.8 fusion.542
  61.2 1.7 bitcast_dynamic-update-slice_fusion.54
  64.9 1.8 fusion.542
  85.2 1.7 bitcast_dynamic-update-slice_fusion.54
  88.9 1.8 fusion.542
  109.1 1.7 bitcast_dynamic-update-slice_fusion.54
  112.8 1.8 fusion.542
  128.5 38.9 %all-reduce.34.cloned.1.call-done = f32[256,1024]{1,0:T(8,128)} async-done(((f32[256,1024]{1,0:T(8,128)}), f32[256,1024]{1,0:T(8,128)}) %all-reduce.34.cloned.1.call-update) | async-done | bytes 1048592 | tf_op jit(solution)/shard_map/psum | solution.py:152
  178.1 36.0 %all-reduce.36.cloned.1.call-done = f32[256,1024]{1,0:T(8,128)} async-done(((f32[256,1024]{1,0:T(8,128)}), f32[256,1024]{1,0:T(8,128)}) %all-reduce.36.cloned.1.call-update) | async-done | bytes 1048592 | tf_op jit(solution)/shard_map/psum | solution.py:173
  214.1 2.3 multiply_reduce_fusion
  226.8 213.1 %while.117 = (s32[]{:T(128)}, f32[2,256,128]{2,1,0:T(8,128)S(1)}, f32[4,64,2,128]{3,1,2,0:T(8,128)}, f32[4,64,2,128]{3,1,2,0:T(8,128)}, f32[4,64,2,256]{3,2,1,0:...) while((s32[]{:T(128)}, f32[2,256,128]{2,1,0:T(8,128)S(1)}, ...), condition=%wide.region_24.25_spmd.clone.clone, body=%wide.region_13.24_spmd.clone.clone.sunk | while | flops 580338304 | bytes 14100944 | solution.py:72
  248.5 1.7 fusion.624
  252.7 1.8 fusion.630
  301.6 1.7 fusion.624
  305.8 1.8 fusion.630
  354.8 1.7 fusion.624
  359.1 1.8 fusion.630
  408.1 1.7 fusion.624
  412.4 1.8 fusion.630
  441.0 1.9 copy.506
  448.9 1.8 multiply_reduce_fusion.15
  465.2 1.7 fusion.256
  469.4 2.0 convolution_add_fusion.15
  471.5 2.6 fusion.322
  477.2 2.7 fusion.280
  480.0 2.0 fusion.300
  482.9 1.9 fusion.299
  486.0 2.1 fusion.327
  489.1 2.1 fusion.328
  492.3 2.2 convolution_bitcast_fusion.7
  495.2 5.9 psum.93
  501.3 30.1 %reduce-scatter.34.cloned.1.call-done = f32[128,2]{1,0:T(8,128)} async-done(((f32[1024,2]{1,0:T(8,128)}), f32[128,2]{1,0:T(8,128)}) %reduce-scatter.34.cloned.1.call-update) | async-done | bytes 1040
  532.9 63.4 %reduce-scatter.36.cloned.1.call-done = f32[128,2]{1,0:T(8,128)} async-done(((f32[1024,2]{1,0:T(8,128)}), f32[128,2]{1,0:T(8,128)}) %reduce-scatter.36.cloned.1.call-update) | async-done | bytes 1040
  597.8 36.0 %all-reduce.38.cloned.1.call-done = f32[256,1024]{1,0:T(8,128)} async-done(((f32[256,1024]{1,0:T(8,128)}), f32[256,1024]{1,0:T(8,128)}) %all-reduce.38.cloned.1.call-update) | async-done | bytes 1048592 | tf_op jit(solution)/shard_map/psum | solution.py:203
  633.8 2.6 multiply_reduce_fusion.1
  636.4 37.7 %all-reduce.29 = (f32[1024]{0:T(1024)}, f32[4,256]{1,0:T(4,128)}, f32[4,256]{1,0:T(4,128)}, f32[4,512]{1,0:T(4,128)}, f32[2]{0:T(128)}, /*index=5*/f32[2]{0:T(128)}, f32[256]{0:T(256)}, f32[1024]{0:T(1024)}) all-reduce(f32[1024]{0:T(1024)S(1)} %get-tuple-element.2794, ...), channel_id=1, replica_groups=mesh['dp'=8,'tensor'=4] {'dp'}, use_global_device_ids=true, to_apply=%region_30.31 | all-reduce | flops 6404 | bytes 51232 | tf_op jit(solution)/shard_map/psum | solution.py:208
  674.1 1.9 dynamic-slice_add_fusion
  675.9 1.8 dynamic-slice_add_fusion.1
  677.7 52.1 %reduce-scatter.20.cloned.1.call-done = f32[128,256]{1,0:T(8,128)} async-done(((f32[1024,256]{1,0:T(8,128)}), f32[128,256]{1,0:T(8,128)}) %reduce-scatter.20.cloned.1.call-update) | async-done | bytes 131088 | tf_op jit(solution)/shard_map/reduce_scatter | solution.py:235
  729.8 67.4 %reduce-scatter.18.cloned.1.call-done = f32[128,256]{1,0:T(8,128)} async-done(((f32[1024,256]{1,0:T(8,128)}), f32[128,256]{1,0:T(8,128)}) %reduce-scatter.18.cloned.1.call-update) | async-done | bytes 131088 | tf_op jit(solution)/shard_map/reduce_scatter | solution.py:234
  797.1 71.6 %reduce-scatter.26.cloned.1.call-done = f32[128,512]{1,0:T(8,128)} async-done(((f32[1024,512]{1,0:T(8,128)}), f32[128,512]{1,0:T(8,128)}) %reduce-scatter.26.cloned.1.call-update) | async-done | bytes 262160 | tf_op jit(solution)/shard_map/reduce_scatter | solution.py:240
  868.7 71.5 %reduce-scatter.22.cloned.1.call-done = f32[128,512]{1,0:T(8,128)} async-done(((f32[1024,512]{1,0:T(8,128)}), f32[128,512]{1,0:T(8,128)}) %reduce-scatter.22.cloned.1.call-update) | async-done | bytes 262160 | tf_op jit(solution)/shard_map/reduce_scatter | solution.py:236
  940.2 71.9 %reduce-scatter.24.cloned.1.call-done = f32[128,512]{1,0:T(8,128)} async-done(((f32[1024,512]{1,0:T(8,128)}), f32[128,512]{1,0:T(8,128)}) %reduce-scatter.24.cloned.1.call-update) | async-done | bytes 262160 | tf_op jit(solution)/shard_map/reduce_scatter | solution.py:237
  1012.1 75.8 %reduce-scatter.28.cloned.1.call-done = f32[128,704]{0,1:T(8,128)} async-done(((f32[1024,704]{0,1:T(8,128)}), f32[128,704]{0,1:T(8,128)}) %reduce-scatter.28.cloned.1.call-update) | async-done | bytes 360464 | tf_op jit(solution)/shard_map/reduce_scatter | solution.py:241
  1087.9 76.2 %reduce-scatter.30.cloned.1.call-done = f32[128,704]{0,1:T(8,128)} async-done(((f32[1024,704]{0,1:T(8,128)}), f32[128,704]{0,1:T(8,128)}) %reduce-scatter.30.cloned.1.call-update) | async-done | bytes 360464 | tf_op jit(solution)/shard_map/reduce_scatter | solution.py:242
  1164.1 76.2 %reduce-scatter.32.cloned.1.call-done = f32[128,704]{0,1:T(8,128)} async-done(((f32[1024,704]{0,1:T(8,128)}), f32[128,704]{0,1:T(8,128)}) %reduce-scatter.32.cloned.1.call-update) | async-done | bytes 360464 | tf_op jit(solution)/shard_map/reduce_scatter | solution.py:243
  (980 shorter events, 358.7 us)
Async XLA Ops:
  7.2 165.6 %copy-start = (bf16[1024,704]{0,1:T(8,128)(2,1)S(1)}, bf16[1024,704]{0,1:T(8,128)(2,1)}, u32[]{:S(2)}) copy-start(bf16[1024,704]{0,1:T(8,128)(2,1)} %param.42) | copy-start | bytes 4325380
  7.2 160.2 %all-reduce.34.cloned.1.call-start = ((), (), s32[]{:S(2)}) async-start(), calls=%async_computation.11 | async-start | bytes 2097152 | tf_op jit(solution)/shard_map/psum | solution.py:152
  8.6 14.5 %copy-start.77 = (f32[256]{0:T(256)}, f32[256]{0:T(256)S(1)}, u32[]{:S(2)}) copy-start(f32[256]{0:T(256)S(1)} %add_rsqrt_fusion.3) | copy-start | bytes 3076
  14.8 8.7 copy-start.64
  14.8 8.8 copy-start.62
  25.4 8.4 copy-start.37
  25.4 10.7 copy-start.26
  48.8 8.0 copy-start.81
  48.8 8.0 copy-start.83
  49.3 8.4 copy-start.37
  49.3 10.7 copy-start.26
  73.3 8.3 copy-start.37
  73.4 10.7 copy-start.26
  97.2 8.3 copy-start.37
  97.2 10.7 copy-start.26
  128.3 40.7 %copy-start.80 = (f32[1024]{0:T(1024)S(1)}, f32[1024]{0:T(1024)}, u32[]{:S(2)}) copy-start(f32[1024]{0:T(1024)} %param.39) | copy-start | bytes 12292
  128.3 85.8 %all-reduce.36.cloned.1.call-start = ((), (), s32[]{:S(2)}) async-start(), calls=%async_computation.13 | async-start | bytes 2097152 | tf_op jit(solution)/shard_map/psum | solution.py:173
  168.9 47.6 %copy-start.2 = (f32[256,1024]{1,0:T(8,128)}, f32[256,1024]{1,0:T(8,128)S(1)}, u32[]{:S(2)}) copy-start(f32[256,1024]{1,0:T(8,128)S(1)} %get-tuple-element.3009) | copy-start | bytes 3145732
  177.2 354.2 %reduce-scatter.34.cloned.1.call-start = ((), (), s32[]{:S(2)}) async-start(), calls=%async_computation.23 | async-start | bytes 589824
  228.1 9.0 copy-start.29
  234.3 9.8 copy-start.28
  234.9 9.7 copy-start.65
  271.1 8.2 copy-start.68
  281.3 9.0 copy-start.29
  287.5 9.8 copy-start.28
  288.1 9.7 copy-start.65
  324.2 8.3 copy-start.68
  334.5 9.0 copy-start.29
  340.7 9.8 copy-start.28
  341.3 9.7 copy-start.65
  377.5 8.3 copy-start.68
  387.8 9.0 copy-start.29
  394.0 9.8 copy-start.28
  394.6 9.7 copy-start.65
  430.8 8.2 copy-start.68
  468.1 128.2 %reduce-scatter.36.cloned.1.call-start = ((), (), s32[]{:S(2)}) async-start(), calls=%async_computation.24 | async-start | bytes 589824
  469.4 164.4 %all-reduce.38.cloned.1.call-start = ((), (), s32[]{:S(2)}) async-start(), calls=%async_computation.14 | async-start | bytes 2097152 | tf_op jit(solution)/shard_map/psum | solution.py:203
  471.5 204.4 %reduce-scatter.16.cloned.1.call-start = ((), (), s32[]{:S(2)}) async-start(), calls=%async_computation.12 | async-start | bytes 1310720 | tf_op jit(solution)/shard_map/reduce_scatter | solution.py:164
  474.1 255.6 %reduce-scatter.20.cloned.1.call-start = ((), (), s32[]{:S(2)}) async-start(), calls=%async_computation.16 | async-start | bytes 1179648 | tf_op jit(solution)/shard_map/reduce_scatter | solution.py:235
  475.7 321.5 %reduce-scatter.18.cloned.1.call-start = ((), (), s32[]{:S(2)}) async-start(), calls=%async_computation.15 | async-start | bytes 1179648 | tf_op jit(solution)/shard_map/reduce_scatter | solution.py:234
  477.2 391.5 %reduce-scatter.26.cloned.1.call-start = ((), (), s32[]{:S(2)}) async-start(), calls=%async_computation.19 | async-start | bytes 2359296 | tf_op jit(solution)/shard_map/reduce_scatter | solution.py:240
  480.0 460.2 %reduce-scatter.22.cloned.1.call-start = ((), (), s32[]{:S(2)}) async-start(), calls=%async_computation.17 | async-start | bytes 2359296 | tf_op jit(solution)/shard_map/reduce_scatter | solution.py:236
  482.0 530.1 %reduce-scatter.24.cloned.1.call-start = ((), (), s32[]{:S(2)}) async-start(), calls=%async_computation.18 | async-start | bytes 2359296 | tf_op jit(solution)/shard_map/reduce_scatter | solution.py:237
  484.9 603.1 %reduce-scatter.28.cloned.1.call-start = ((), (), s32[]{:S(2)}) async-start(), calls=%async_computation.20 | async-start | bytes 3244032 | tf_op jit(solution)/shard_map/reduce_scatter | solution.py:241
  488.1 676.0 %reduce-scatter.30.cloned.1.call-start = ((), (), s32[]{:S(2)}) async-start(), calls=%async_computation.21 | async-start | bytes 3244032 | tf_op jit(solution)/shard_map/reduce_scatter | solution.py:242
  491.2 749.2 %reduce-scatter.32.cloned.1.call-start = ((), (), s32[]{:S(2)}) async-start(), calls=%async_computation.22 | async-start | bytes 3244032 | tf_op jit(solution)/shard_map/reduce_scatter | solution.py:243
  597.8 38.6 %copy-start.101 = (f32[1024]{0:T(1024)S(1)}, f32[1024]{0:T(1024)}, u32[]{:S(2)}) copy-start(f32[1024]{0:T(1024)} %get-tuple-element.2786) | copy-start | bytes 12292
  597.8 38.6 %copy-start.141 = (f32[2]{0:T(128)S(1)}, f32[2]{0:T(128)}, u32[]{:S(2)}) copy-start(f32[2]{0:T(128)} %get-tuple-element.2998) | copy-start | bytes 28
  (177 other events, 595.7 us)
Sparse Core Ops, SparseCore 0:
  128.4 39.0 all-reduce.33
  177.4 36.7 all-reduce.35
  468.2 63.1 reduce-scatter.33
  534.6 61.6 reduce-scatter.35
  598.5 35.2 all-reduce.37
  636.2 25.2 reduce-scatter.15
  665.5 64.2 reduce-scatter.19
  733.7 63.3 reduce-scatter.17
  801.2 67.4 reduce-scatter.25
  872.6 67.4 reduce-scatter.21
  944.3 67.7 reduce-scatter.23
  1016.1 71.8 reduce-scatter.27
  1092.1 72.0 reduce-scatter.29
  1168.1 72.1 reduce-scatter.31
where the time goes:
time: 1250 us
  waiting for transfers between devices  767 us (61%)
  matrix products  230 us (18%)
  local copies, waits for them, and re-layouts  107 us (9%)
  other arithmetic  80.2 us (6%)
  blocking collectives  43.6 us (3%)
  between operations  15.7 us (1%)
    unnamed x16, waiting for transfers between devices  93.8 us
    reduce_scatter x1, waiting for transfers between devices, local(): lax.psum_scatter(grad_down, 'dp', scatter_dimension=0, tiled=True)  76.2 us
    reduce_scatter x1, waiting for transfers between devices, local(): lax.psum_scatter(grad_up, 'dp', scatter_dimension=0, tiled=True)  76.2 us
    reduce_scatter x1, waiting for transfers between devices, local(): lax.psum_scatter(grad_gate, 'dp', scatter_dimension=0, tiled=True)  75.8 us
    reduce_scatter x1, waiting for transfers between devices, local(): lax.psum_scatter(grad_outgate, 'dp', scatter_dimension=0, tiled=True)  71.9 us
    reduce_scatter x1, waiting for transfers between devices, local(): lax.psum_scatter(grad_out, 'dp', scatter_dimension=0, tiled=True)  71.6 us
    reduce_scatter x1, waiting for transfers between devices, local(): lax.psum_scatter(grad_value, 'dp', scatter_dimension=0, tiled=True)  71.5 us
    reduce_scatter x1, waiting for transfers between devices, local(): lax.psum_scatter(grad_query, 'dp', scatter_dimension=0, tiled=True)  67.4 us
  transfers between devices with their start and end apart: 14, of which 13 were waited for; matrix products, arithmetic and copies ran while one was open for 3% of the time, Pallas kernels for 0%

commit v1 on v0

--- a/solution.py
+++ b/solution.py
@@ -170,7 +170,7 @@
     grad_gate = outer_sum(normed_second, dglin)
     grad_up = outer_sum(normed_second, dulin)
     second_part = back_dot(dglin, w_gate) + back_dot(dulin, w_up)
-    dnormed2 = lax.psum(second_part, "tensor")
+    dnormed2 = lax.all_gather(second_part, "tensor").sum(axis=0)
     grad_ffn_gain = jnp.sum(dnormed2 * unit_second, axis=0)
     dresid = cotangent.astype(jnp.float32) + rms_back(dnormed2, unit_second, inv_second, ffn_gain)
     dresid_bf = dresid.astype(jnp.bfloat16)

time: 1250 us -> 1160 us (0.928)
  waiting for transfers between devices: 767 us -> 731 us
  other arithmetic: 80.2 us -> 52.9 us
  local copies, waits for them, and re-layouts: 107 us -> 82.2 us
  matrix products: 230 us -> 210 us
    reduce_scatter x1, waiting for transfers between devices: 75.8 us -> 34 us  [local(): lax.psum_scatter(grad_gate, 'dp', scatter_dimension=0, tiled=True)]
    psum x1 -> x0, waiting for transfers between devices: 36 us -> none  [local(): dnormed2 = lax.psum(second_part, 'tensor')]
    all_gather x0 -> x1, waiting for transfers between devices: none -> 32.5 us  [local(): dnormed2 = lax.all_gather(second_part, 'tensor').sum(axis=0)]
    reduce_scatter x1, waiting for transfers between devices: 52.1 us -> 67.3 us  [local(): lax.psum_scatter(grad_key, 'dp', scatter_dimension=0, tiled=True)]
  transfers between devices with their start and end apart: 14 -> 14, of which waited for: 13 -> 13; matrix products, arithmetic and copies ran while one was open for 3% -> 17% of each run, Pallas kernels for 0% -> 0%
where the time goes in v1:
time: 1160 us; the launch traced here: 1150 us
  waiting for transfers between devices  731 us (63%)
  matrix products  210 us (18%)
  local copies, waits for them, and re-layouts  82.2 us (7%)
  other arithmetic  52.9 us (5%)
  blocking collectives  45 us (4%)
  between operations  16.3 us (1%)
    unnamed x16, waiting for transfers between devices  97.5 us
    reduce_scatter x1, waiting for transfers between devices, local(): lax.psum_scatter(grad_up, 'dp', scatter_dimension=0, tiled=True)  76.2 us
    reduce_scatter x1, waiting for transfers between devices, local(): lax.psum_scatter(grad_down, 'dp', scatter_dimension=0, tiled=True)  76.2 us
    reduce_scatter x1, waiting for transfers between devices, local(): lax.psum_scatter(grad_out, 'dp', scatter_dimension=0, tiled=True)  71.5 us
    reduce_scatter x1, waiting for transfers between devices, local(): lax.psum_scatter(grad_value, 'dp', scatter_dimension=0, tiled=True)  71.5 us
    reduce_scatter x1, waiting for transfers between devices, local(): lax.psum_scatter(grad_outgate, 'dp', scatter_dimension=0, tiled=True)  71.4 us
    reduce_scatter x1, waiting for transfers between devices, local(): lax.psum_scatter(grad_query, 'dp', scatter_dimension=0, tiled=True)  67.3 us
    reduce_scatter x1, waiting for transfers between devices, local(): lax.psum_scatter(grad_key, 'dp', scatter_dimension=0, tiled=True)  67.3 us
  transfers between devices with their start and end apart: 14, of which 13 were waited for; matrix products, arithmetic and copies ran while one was open for 17% of the time, Pallas kernels for 0%

profile of v1, /device:TPU:0, one launch (start us, length us, event | category | flops | bytes accessed | tf_op | source)
XLA Modules:
  0.0 1149.2 jit_solution(3605929312712483802)
XLA Ops:
  9.5 1.6 fusion.306
  20.3 1.7 fusion.305
  28.9 103.5 %while.116 = (s32[]{:T(128)}, f32[2,256,128]{2,1,0:T(8,128)S(1)}, f32[4,64,2,256]{3,1,2,0:T(8,128)}, f32[4,64,64,2]{1,2,3,0:T(8,128)}, f32[4,64,2]{1,2,0:T(2,128...) while((s32[]{:T(128)}, f32[2,256,128]{2,1,0:T(8,128)S(1)}, ...), condition=%wide.region_5.6_spmd.clone.clone, body=%wide.region_3.5_spmd.clone.clone.sunk | while | flops 290349312 | bytes 8164578 | solution.py:72
  41.5 1.8 bitcast_dynamic-update-slice_fusion.53
  43.3 1.7 bitcast_dynamic-update-slice_fusion.54
  46.9 1.8 fusion.542
  67.3 1.8 bitcast_dynamic-update-slice_fusion.53
  69.2 1.7 bitcast_dynamic-update-slice_fusion.54
  72.8 1.7 fusion.542
  93.3 1.8 bitcast_dynamic-update-slice_fusion.53
  95.1 1.7 bitcast_dynamic-update-slice_fusion.54
  98.8 1.7 fusion.542
  119.2 1.8 bitcast_dynamic-update-slice_fusion.53
  121.0 1.6 bitcast_dynamic-update-slice_fusion.54
  124.6 1.7 fusion.542
  133.6 1.4 copy.477
  140.0 9.8 all-gather.3.cloned.1.call-start
  149.8 29.3 %all-reduce.33.cloned.1.call-done = f32[256,1024]{1,0:T(8,128)} async-done(((f32[256,1024]{1,0:T(8,128)}), f32[256,1024]{1,0:T(8,128)}) %all-reduce.33.cloned.1.call-update) | async-done | bytes 1048592 | tf_op jit(solution)/shard_map/psum | solution.py:152
  180.8 1.5 copy-done.11
  186.5 1.6 convolution_add_fusion.18
  189.0 1.6 fusion.322
  190.7 32.5 %all-gather.3.cloned.1.call-done = f32[1024,1024]{1,0:T(8,128)} async-done(((f32[256,1024]{1,0:T(8,128)}), f32[1024,1024]{1,0:T(8,128)}) %all-gather.3.cloned.1.call-update) | async-done | bytes 4194320 | tf_op jit(solution)/shard_map/all_gather | solution.py:173
  223.2 2.8 reduce_sum.527
  236.1 144.3 %while.117 = (s32[]{:T(128)}, f32[2,256,128]{2,1,0:T(8,128)S(1)}, f32[4,64,2,128]{3,1,2,0:T(8,128)}, f32[4,64,2,128]{3,1,2,0:T(8,128)}, f32[4,64,2,256]{3,2,1,0:...) while((s32[]{:T(128)}, f32[2,256,128]{2,1,0:T(8,128)S(1)}, ...), condition=%wide.region_24.25_spmd.clone.clone, body=%wide.region_13.24_spmd.clone.clone.sunk | while | flops 580338304 | bytes 14117188 | solution.py:72
  401.2 2.1 fusion.327
  404.2 2.2 fusion.328
  407.5 2.2 convolution_bitcast_fusion.7
  412.8 1.8 fusion.280
  414.7 1.9 fusion.300
  416.6 2.0 fusion.299
  418.8 1.8 dynamic-slice_add_fusion.1
  420.6 6.3 psum.85
  427.0 33.9 %reduce-scatter.34.cloned.1.call-done = f32[128,2]{1,0:T(8,128)} async-done(((f32[1024,2]{1,0:T(8,128)}), f32[128,2]{1,0:T(8,128)}) %reduce-scatter.34.cloned.1.call-update) | async-done | bytes 1040
  460.9 1.5 copy.540
  462.4 63.4 %reduce-scatter.36.cloned.1.call-done = f32[128,2]{1,0:T(8,128)} async-done(((f32[1024,2]{1,0:T(8,128)}), f32[128,2]{1,0:T(8,128)}) %reduce-scatter.36.cloned.1.call-update) | async-done | bytes 1040
  525.8 1.5 copy.542
  527.3 36.1 %all-reduce.35.cloned.1.call-done = f32[256,1024]{1,0:T(8,128)} async-done(((f32[256,1024]{1,0:T(8,128)}), f32[256,1024]{1,0:T(8,128)}) %all-reduce.35.cloned.1.call-update) | async-done | bytes 1048592 | tf_op jit(solution)/shard_map/psum | solution.py:203
  563.3 3.0 multiply_reduce_fusion.1
  566.3 38.7 %all-reduce.29 = (f32[1024]{0:T(1024)}, f32[4,256]{1,0:T(4,128)}, f32[4,256]{1,0:T(4,128)}, f32[4,512]{1,0:T(4,128)}, f32[2]{0:T(128)}, /*index=5*/f32[2]{0:T(128)}, f32[256]{0:T(256)}, f32[1024]{0:T(1024)}) all-reduce(f32[1024]{0:T(1024)S(1)} %get-tuple-element.2794, ...), channel_id=1, replica_groups=mesh['dp'=8,'tensor'=4] {'dp'}, use_global_device_ids=true, to_apply=%region_30.31 | all-reduce | flops 6404 | bytes 51232 | tf_op jit(solution)/shard_map/psum | solution.py:208
  605.1 1.9 dynamic-slice_add_fusion
  606.9 34.0 %reduce-scatter.28.cloned.1.call-done = f32[128,704]{0,1:T(8,128)} async-done(((f32[1024,704]{0,1:T(8,128)}), f32[128,704]{0,1:T(8,128)}) %reduce-scatter.28.cloned.1.call-update) | async-done | bytes 360464 | tf_op jit(solution)/shard_map/reduce_scatter | solution.py:241
  641.0 76.2 %reduce-scatter.30.cloned.1.call-done = f32[128,704]{0,1:T(8,128)} async-done(((f32[1024,704]{0,1:T(8,128)}), f32[128,704]{0,1:T(8,128)}) %reduce-scatter.30.cloned.1.call-update) | async-done | bytes 360464 | tf_op jit(solution)/shard_map/reduce_scatter | solution.py:242
  717.2 76.2 %reduce-scatter.32.cloned.1.call-done = f32[128,704]{0,1:T(8,128)} async-done(((f32[1024,704]{0,1:T(8,128)}), f32[128,704]{0,1:T(8,128)}) %reduce-scatter.32.cloned.1.call-update) | async-done | bytes 360464 | tf_op jit(solution)/shard_map/reduce_scatter | solution.py:243
  793.3 67.3 %reduce-scatter.20.cloned.1.call-done = f32[128,256]{1,0:T(8,128)} async-done(((f32[1024,256]{1,0:T(8,128)}), f32[128,256]{1,0:T(8,128)}) %reduce-scatter.20.cloned.1.call-update) | async-done | bytes 131088 | tf_op jit(solution)/shard_map/reduce_scatter | solution.py:235
  860.6 67.3 %reduce-scatter.18.cloned.1.call-done = f32[128,256]{1,0:T(8,128)} async-done(((f32[1024,256]{1,0:T(8,128)}), f32[128,256]{1,0:T(8,128)}) %reduce-scatter.18.cloned.1.call-update) | async-done | bytes 131088 | tf_op jit(solution)/shard_map/reduce_scatter | solution.py:234
  927.9 71.5 %reduce-scatter.26.cloned.1.call-done = f32[128,512]{1,0:T(8,128)} async-done(((f32[1024,512]{1,0:T(8,128)}), f32[128,512]{1,0:T(8,128)}) %reduce-scatter.26.cloned.1.call-update) | async-done | bytes 262160 | tf_op jit(solution)/shard_map/reduce_scatter | solution.py:240
  999.4 71.5 %reduce-scatter.22.cloned.1.call-done = f32[128,512]{1,0:T(8,128)} async-done(((f32[1024,512]{1,0:T(8,128)}), f32[128,512]{1,0:T(8,128)}) %reduce-scatter.22.cloned.1.call-update) | async-done | bytes 262160 | tf_op jit(solution)/shard_map/reduce_scatter | solution.py:236
  1070.9 71.4 %reduce-scatter.24.cloned.1.call-done = f32[128,512]{1,0:T(8,128)} async-done(((f32[1024,512]{1,0:T(8,128)}), f32[128,512]{1,0:T(8,128)}) %reduce-scatter.24.cloned.1.call-update) | async-done | bytes 262160 | tf_op jit(solution)/shard_map/reduce_scatter | solution.py:237
  (915 shorter events, 290.8 us)
Async XLA Ops:
  7.2 177.3 %copy-start = (bf16[1024,704]{0,1:T(8,128)(2,1)S(1)}, bf16[1024,704]{0,1:T(8,128)(2,1)}, u32[]{:S(2)}) copy-start(bf16[1024,704]{0,1:T(8,128)(2,1)} %param.42) | copy-start | bytes 4325380
  7.2 171.9 %all-reduce.33.cloned.1.call-start = ((), (), s32[]{:S(2)}) async-start(), calls=%async_computation.11 | async-start | bytes 2097152 | tf_op jit(solution)/shard_map/psum | solution.py:152
  8.6 18.1 %copy-start.73 = (f32[256]{0:T(256)}, f32[256]{0:T(256)S(1)}, u32[]{:S(2)}) copy-start(f32[256]{0:T(256)S(1)} %add_rsqrt_fusion.3) | copy-start | bytes 3076
  15.6 12.2 %copy-start.64 = (pred[64,64]{1,0:T(8,128)(4,1)}, pred[64,64]{1,0:T(8,128)(4,1)S(1)}, u32[]{:S(2)}) copy-start(pred[64,64]{1,0:T(8,128)(4,1)S(1)} %get-tuple-element.3993) | copy-start | bytes 12292
  30.8 8.3 copy-start.28
  56.6 8.2 copy-start.28
  82.5 8.3 copy-start.28
  108.5 8.3 copy-start.28
  135.1 95.7 %copy-start.76 = (f32[4,64,2]{1,2,0:T(2,128)}, f32[4,64,2]{1,2,0:T(2,128)S(1)}, u32[]{:S(2)}) copy-start(f32[4,64,2]{1,2,0:T(2,128)S(1)} %fusion.287) | copy-start | bytes 6148
  140.0 40.6 %copy-start.79 = (f32[1024]{0:T(1024)S(1)}, f32[1024]{0:T(1024)}, u32[]{:S(2)}) copy-start(f32[1024]{0:T(1024)} %param.39) | copy-start | bytes 12292
  140.0 83.2 %all-gather.3.cloned.1.call-start = ((), (), s32[]{:S(2)}) async-start(), calls=%async_computation.22 | async-start | bytes 5242880 | tf_op jit(solution)/shard_map/all_gather | solution.py:173
  188.1 230.6 %reduce-scatter.16.cloned.1.call-start = ((), (), s32[]{:S(2)}) async-start(), calls=%async_computation.12 | async-start | bytes 1310720 | tf_op jit(solution)/shard_map/reduce_scatter | solution.py:164
  190.6 270.3 %reduce-scatter.34.cloned.1.call-start = ((), (), s32[]{:S(2)}) async-start(), calls=%async_computation.23 | async-start | bytes 589824
  236.2 7.6 copy-start.32
  237.5 9.0 copy-start.31
  243.7 9.8 copy-start.30
  272.1 7.6 copy-start.32
  273.4 9.0 copy-start.31
  279.7 9.8 copy-start.30
  309.5 9.0 copy-start.31
  315.8 9.8 copy-start.30
  344.3 7.6 copy-start.32
  345.6 9.0 copy-start.31
  351.8 9.8 copy-start.30
  398.1 127.7 %reduce-scatter.36.cloned.1.call-start = ((), (), s32[]{:S(2)}) async-start(), calls=%async_computation.24 | async-start | bytes 589824
  399.7 163.7 %all-reduce.35.cloned.1.call-start = ((), (), s32[]{:S(2)}) async-start(), calls=%async_computation.13 | async-start | bytes 2097152 | tf_op jit(solution)/shard_map/psum | solution.py:203
  401.1 239.8 %reduce-scatter.28.cloned.1.call-start = ((), (), s32[]{:S(2)}) async-start(), calls=%async_computation.19 | async-start | bytes 3244032 | tf_op jit(solution)/shard_map/reduce_scatter | solution.py:241
  403.3 313.9 %reduce-scatter.30.cloned.1.call-start = ((), (), s32[]{:S(2)}) async-start(), calls=%async_computation.20 | async-start | bytes 3244032 | tf_op jit(solution)/shard_map/reduce_scatter | solution.py:242
  406.4 386.9 %reduce-scatter.32.cloned.1.call-start = ((), (), s32[]{:S(2)}) async-start(), calls=%async_computation.21 | async-start | bytes 3244032 | tf_op jit(solution)/shard_map/reduce_scatter | solution.py:243
  409.7 450.8 %reduce-scatter.20.cloned.1.call-start = ((), (), s32[]{:S(2)}) async-start(), calls=%async_computation.15 | async-start | bytes 1179648 | tf_op jit(solution)/shard_map/reduce_scatter | solution.py:235
  411.3 516.6 %reduce-scatter.18.cloned.1.call-start = ((), (), s32[]{:S(2)}) async-start(), calls=%async_computation.14 | async-start | bytes 1179648 | tf_op jit(solution)/shard_map/reduce_scatter | solution.py:234
  412.8 586.6 %reduce-scatter.26.cloned.1.call-start = ((), (), s32[]{:S(2)}) async-start(), calls=%async_computation.18 | async-start | bytes 2359296 | tf_op jit(solution)/shard_map/reduce_scatter | solution.py:240
  414.7 656.2 %reduce-scatter.22.cloned.1.call-start = ((), (), s32[]{:S(2)}) async-start(), calls=%async_computation.16 | async-start | bytes 2359296 | tf_op jit(solution)/shard_map/reduce_scatter | solution.py:236
  416.6 725.7 %reduce-scatter.24.cloned.1.call-start = ((), (), s32[]{:S(2)}) async-start(), calls=%async_computation.17 | async-start | bytes 2359296 | tf_op jit(solution)/shard_map/reduce_scatter | solution.py:237
  418.6 8.3 copy-start.126
  418.6 8.3 copy-start.127
  418.6 8.3 copy-start.128
  418.6 8.3 copy-start.129
  418.6 8.3 copy-start.130
  418.6 8.3 copy-start.131
  418.7 8.3 copy-start.132
  418.7 8.3 copy-start.133
  418.7 8.3 copy-start.120
  418.7 8.3 copy-start.121
  418.7 8.3 copy-start.143
  527.3 39.1 %copy-start.98 = (f32[1024]{0:T(1024)S(1)}, f32[1024]{0:T(1024)}, u32[]{:S(2)}) copy-start(f32[1024]{0:T(1024)} %get-tuple-element.2786) | copy-start | bytes 12292
  527.3 39.1 %copy-start.138 = (f32[2]{0:T(128)S(1)}, f32[2]{0:T(128)}, u32[]{:S(2)}) copy-start(f32[2]{0:T(128)} %get-tuple-element.2998) | copy-start | bytes 28
  563.3 579.0 %copy-start.1 = (bf16[1024,704]{0,1:T(8,128)(2,1)S(1)}, bf16[1024,704]{0,1:T(8,128)(2,1)}, u32[]{:S(2)}) copy-start(bf16[1024,704]{0,1:T(8,128)(2,1)} %param.42) | copy-start | bytes 4325380
  (144 other events, 341.2 us)
Sparse Core Ops, SparseCore 0:
  140.1 38.9 all-reduce.32
  188.3 34.9 all-gather.2
  225.8 24.7 reduce-scatter.15
  398.2 62.6 reduce-scatter.33
  464.1 61.6 reduce-scatter.35
  528.0 35.2 all-reduce.34
  567.4 73.4 reduce-scatter.27
  645.1 72.0 reduce-scatter.29
  721.3 71.9 reduce-scatter.31
  797.1 63.3 reduce-scatter.19
  864.6 63.2 reduce-scatter.17
  931.8 67.5 reduce-scatter.25
  1003.5 67.3 reduce-scatter.21
  1074.8 67.4 reduce-scatter.23
